TPU v7x, 512 devices: a whole 4x4x16 slice. The times are simulated.
512 devices in a mesh: kv: 8 (over x, core), pool: 64 (over y, z).
Axes of the slice: x: 4, y: 4, z: 16, core: 2. Of those that a mesh axis runs over, the one named last changes fastest.
Arguments:
- hidden: bfloat16 [64, 2048], P('pool'), may hold values from -6 to 6
- norm_attn: bfloat16 [2048], replicated, may hold values from 0.099609375 to 1.8984375
- wq: bfloat16 [2048, 2048], P(None, 'kv'), may hold values from -0.125 to 0.125
- wkv: bfloat16 [2, 2048, 1024], P(None, None, 'kv'), may hold values from -0.125 to 0.125
- wo: bfloat16 [2048, 2048], P('kv'), may hold values from -0.125 to 0.125
- cache: bfloat16 [2, 1024, 128, 1024], P(None, 'pool', None, 'kv'), may hold values from -70 to 70, as said below
- slot_entry: int32 [1024], P('pool'), may hold values from -1 to 4095, as said below
- lengths: int32 [64], replicated, may hold values from 1 to 8192, as said below
- norm_mlp: bfloat16 [2048], replicated, may hold values from 0.099609375 to 1.8984375
- w_gate: bfloat16 [2048, 8192], P('pool', 'kv'), may hold values from -0.125 to 0.125
- w_up: bfloat16 [2048, 8192], P('pool', 'kv'), may hold values from -0.125 to 0.125
- w_down: bfloat16 [8192, 2048], P('kv', 'pool'), may hold values from -0.0625 to 0.0625
Outputs:
- output: bfloat16 [64, 2048], P('pool')
Inputs may be any that keep to these rules, and one draw needn't show every extreme that they name: slot_entry[s] is -1 for a free slot, else r * 64 + b: the slot holds block b of request r, that is its cached positions b * 128 to b * 128 + 127 that lie below lengths[r]. Every block of every request below ceil(lengths[r] / 128) sits in exactly one slot, anywhere in the pool; a holder's slots are its 16 entries. Its new token stands at position lengths[r]. `cache`: keys and values of the cached tokens, already rotated.
All inputs are finite; a program needn't handle non-finite values.
Results may differ from a plain program's by a relative error of at most 0.012.
The roundings to bfloat16 on the way count: a program that leaves them out, or rounds other values in their place, can miss the bound.
Values may be sent and summed in bfloat16 or wider, within the bound.
A program may use at most 64 MiB of HBM per device.

v0:
```python
import math
import jax
import jax.numpy as jnp
from jax import lax
from jax.sharding import PartitionSpec as P

QUERY_HEAD_COUNT = 16
KEY_VALUE_HEADS = 8
HEAD_SIZE = 128
NEGATIVE = -1e30
EPSILON = 1e-05
ROPE_BASE = 1000000.0


def combined_all(x, axis, combine):
    everything = jax.tree.map(lambda part: lax.all_gather(part, axis), x)
    initial = jax.tree.map(lambda part: part[0], everything)

    def step(k, so_far):
        return combine(so_far, jax.tree.map(lambda part: part[k], everything))

    return lax.fori_loop(1, lax.axis_size(axis), step, initial)


def narrow_rows(tensor):
    return lax.optimization_barrier(tensor.astype(jnp.bfloat16))


def rms_scale(inputs, gain_vec):
    widened = inputs.astype(jnp.float32)
    mean_square = jnp.mean(widened * widened, axis=-1, keepdims=True)
    return narrow_rows(widened * lax.rsqrt(mean_square + EPSILON) * gain_vec.astype(jnp.float32))


def rotate(vectors, positions):
    head_width = vectors.shape[-1]
    halfway = head_width // 2
    frequency = jnp.exp(
        jnp.arange(halfway, dtype=jnp.float32) * (-2.0 * math.log(ROPE_BASE) / head_width)
    )
    angles = positions.astype(jnp.float32)[:, None] * frequency[None, :]
    cosine = jnp.cos(angles)[:, None, :]
    sine_of = jnp.sin(angles)[:, None, :]
    leading = vectors[..., :halfway]
    trailing = vectors[..., halfway:]
    return jnp.concatenate(
        [leading * cosine - trailing * sine_of, trailing * cosine + leading * sine_of], axis=-1
    )


def combine(earlier, latter):
    highest = jnp.maximum(earlier[0], latter[0])
    scale_early = jnp.exp(earlier[0] - highest)
    scale_late = jnp.exp(latter[0] - highest)
    row_count, head_count = highest.shape
    feature = earlier[2].shape[1] // head_count
    early_out = earlier[2].reshape(row_count, head_count, feature) * scale_early[:, :, None]
    late_out = latter[2].reshape(row_count, head_count, feature) * scale_late[:, :, None]
    weight_sum = earlier[1] * scale_early + latter[1] * scale_late
    return (highest, weight_sum, (early_out + late_out).reshape(row_count, head_count * feature))


def per_device(
    hidden, norm_attn, wq, wkv, wo, cache, slot_entry, lengths, norm_mlp, w_gate, w_up, w_down
):
    home_rows = hidden.shape[0]
    shared_heads = wkv.shape[2] // HEAD_SIZE
    queries_per_shared = QUERY_HEAD_COUNT // KEY_VALUE_HEADS
    query_heads = shared_heads * queries_per_shared
    home_index = lax.axis_index("pool")
    max_blocks = slot_entry.shape[0] * lax.axis_size("pool") // 16
    positions = lax.dynamic_slice_in_dim(lengths, home_index * home_rows, home_rows)
    normed_input = rms_scale(hidden, norm_attn)
    query_rows = jnp.dot(normed_input, wq, preferred_element_type=jnp.float32).reshape(
        home_rows, query_heads, HEAD_SIZE
    )
    query_rows = narrow_rows(rotate(query_rows, positions) * HEAD_SIZE ** (-0.5))
    fresh_keys = jnp.dot(normed_input, wkv[0], preferred_element_type=jnp.float32).reshape(
        home_rows, shared_heads, HEAD_SIZE
    )
    fresh_keys = narrow_rows(rotate(fresh_keys, positions))
    fresh_values = narrow_rows(
        jnp.dot(normed_input, wkv[1], preferred_element_type=jnp.float32)
    ).reshape(home_rows, shared_heads, HEAD_SIZE)
    every_query = lax.all_gather(
        query_rows.reshape(home_rows, query_heads * HEAD_SIZE), "pool", axis=0, tiled=True
    )
    request_list = every_query.shape[0]
    every_query = every_query.reshape(request_list, shared_heads, queries_per_shared, HEAD_SIZE)
    slot_count = slot_entry.shape[0]
    block_len = cache.shape[2]
    live_slot = slot_entry >= 0
    owners = jnp.where(live_slot, slot_entry // max_blocks, 0)
    block_index = jnp.where(live_slot, slot_entry % max_blocks, 0)
    picked = every_query[owners]
    block_keys = cache[0].reshape(slot_count, block_len, shared_heads, HEAD_SIZE)
    block_values = cache[1].reshape(slot_count, block_len, shared_heads, HEAD_SIZE)
    scores = jnp.einsum("sgjd,stgd->sgjt", picked, block_keys, preferred_element_type=jnp.float32)
    position = block_index[:, None] * block_len + jnp.arange(block_len, dtype=jnp.int32)[None, :]
    in_range = live_slot[:, None] & (position < lengths[owners][:, None])
    scores = jnp.where(in_range[:, None, None, :], scores, NEGATIVE)
    block_max = jnp.max(scores, axis=-1)
    same_owner = (owners[:, None] == owners[None, :]) & live_slot[:, None] & live_slot[None, :]
    holder_max = jnp.max(jnp.where(same_owner[:, :, None, None], block_max[None], NEGATIVE), axis=1)
    raised = jnp.where(in_range[:, None, None, :], jnp.exp(scores - holder_max[..., None]), 0.0)
    holder_total = jnp.sum(raised, axis=-1)
    holder_output = jnp.einsum(
        "sgjt,stgd->sgjd", narrow_rows(raised), block_values, preferred_element_type=jnp.float32
    )
    member = (owners[:, None] == jnp.arange(request_list, dtype=jnp.int32)[None, :]) & live_slot[
        :, None
    ]
    request_max = jnp.max(jnp.where(member.T[:, :, None, None], holder_max[None], NEGATIVE), axis=1)
    request_max = request_max.reshape(request_list, query_heads)
    member_float = member.astype(jnp.float32)
    request_total = jnp.einsum(
        "sr,sgj->rgj", member_float, holder_total, precision=lax.Precision.HIGHEST
    )
    request_total = request_total.reshape(request_list, query_heads)
    request_out = jnp.einsum(
        "sr,sgjd->rgjd", member_float, holder_output, precision=lax.Precision.HIGHEST
    )
    request_out = request_out.reshape(request_list, query_heads * HEAD_SIZE)
    merged = combined_all((request_max, request_total, request_out), "pool", combine)
    part_max = lax.dynamic_slice_in_dim(merged[0], home_index * home_rows, home_rows)
    part_total = lax.dynamic_slice_in_dim(merged[1], home_index * home_rows, home_rows)
    part_out = lax.dynamic_slice_in_dim(merged[2], home_index * home_rows, home_rows)
    own_query = query_rows.reshape(home_rows, shared_heads, queries_per_shared, HEAD_SIZE).astype(
        jnp.float32
    )
    new_score = jnp.sum(own_query * fresh_keys.astype(jnp.float32)[:, :, None, :], axis=-1).reshape(
        home_rows, query_heads
    )
    highest = jnp.maximum(part_max, new_score)
    old_scale = jnp.exp(part_max - highest)
    new_scale = jnp.exp(new_score - highest)
    weight_sum = part_total * old_scale + new_scale
    new_term = (
        new_scale.reshape(home_rows, shared_heads, queries_per_shared)[..., None]
        * fresh_values.astype(jnp.float32)[:, :, None, :]
    )
    combined = part_out.reshape(home_rows, query_heads, HEAD_SIZE) * old_scale[
        ..., None
    ] + new_term.reshape(home_rows, query_heads, HEAD_SIZE)
    attended = narrow_rows(combined / weight_sum[..., None]).reshape(
        home_rows, query_heads * HEAD_SIZE
    )
    projected = lax.psum(jnp.dot(attended, wo, preferred_element_type=jnp.float32), "kv")
    residual = narrow_rows(hidden.astype(jnp.float32) + projected)
    mlp_in = rms_scale(residual, norm_mlp)
    columns = lax.all_to_all(mlp_in, "pool", split_axis=1, concat_axis=0, tiled=True)
    hidden_width = w_gate.shape[1]
    gate_term = jnp.dot(columns, w_gate, preferred_element_type=jnp.float32)
    up_term = jnp.dot(columns, w_up, preferred_element_type=jnp.float32)
    summed = lax.psum_scatter(
        jnp.concatenate([gate_term, up_term], axis=1), "pool", scatter_dimension=0, tiled=True
    )
    activation = narrow_rows(jax.nn.silu(summed[:, :hidden_width]) * summed[:, hidden_width:])
    projected_down = jnp.dot(
        lax.all_gather(activation, "pool", axis=0, tiled=True),
        w_down,
        preferred_element_type=jnp.float32,
    )
    mlp_out = narrow_rows(lax.psum(projected_down, "kv"))
    returned = lax.all_to_all(mlp_out, "pool", split_axis=0, concat_axis=1, tiled=True)
    return (residual.astype(jnp.float32) + returned.astype(jnp.float32)).astype(jnp.bfloat16)


def solution(mesh):
    return jax.shard_map(
        per_device,
        mesh=mesh,
        in_specs=(
            P("pool", None),
            P(),
            P(None, "kv"),
            P(None, None, "kv"),
            P("kv", None),
            P(None, "pool", None, "kv"),
            P("pool"),
            P(),
            P(),
            P("pool", "kv"),
            P("pool", "kv"),
            P("kv", "pool"),
        ),
        out_specs=P("pool", None),
        check_vma=False,
    )
```

profile of v0, /device:TPU:8, one launch (start us, length us, event | category | flops | bytes accessed | tf_op | source)
XLA Modules:
  0.0 794.5 jit_solution(5610471597167837660)
XLA Ops:
  8.0 1.2 dynamic_slice.42
  10.6 1.3 multiply_reduce_fusion.1
  13.3 1.5 fusion.5
  15.0 88.2 %all-gather.3 = bf16[64,1,256]{2,1,0:T(2,128)(2,1)S(1)} all-gather(bf16[1,1,256]{2,1,0:T(2,128)(2,1)S(1)} %reshape.618), channel_id=1, replica_groups=mesh['kv'=8,'pool'=64] {'pool'}, dimensions={0}, use_global_device_ids=true | all-gather | bytes 33280 | tf_op jit(solution)/shard_map/all_gather | solution.py:85
  103.4 1.3 gather_fusion
  105.5 1.5 fusion.61
  107.5 1.3 fusion.10
  108.8 0.9 fusion.20
  109.8 1.2 convolution_bitcast_fusion.2
  111.2 1.2 fusion.4
  112.6 79.4 %all-gather.5 = f32[64,64,2]{1,2,0:T(2,128)S(1)} all-gather(f32[1,64,2]{1,2,0:T(2,128)S(1)} %convolution_bitcast_fusion), channel_id=3, replica_groups=mesh['kv'=8,'pool'=64] {'pool'}, dimensions={0}, use_global_device_ids=true | all-gather | bytes 33280 | tf_op jit(solution)/shard_map/all_gather | solution.py:16
  192.2 81.0 %all-gather.4 = f32[64,64,2]{1,2,0:T(2,128)S(1)} all-gather(f32[1,64,2]{1,2,0:T(2,128)S(1)} %bitcast.156), channel_id=2, replica_groups=mesh['kv'=8,'pool'=64] {'pool'}, dimensions={0}, use_global_device_ids=true | all-gather | bytes 33280 | tf_op jit(solution)/shard_map/all_gather | solution.py:16
  274.2 87.2 %while.19 = (s32[]{:T(128)}, f32[64,2]{0,1:T(2,128)S(1)}, f32[64,2]{0,1:T(2,128)S(1)}, f32[64,256]{1,0:T(8,128)S(1)}, f32[64,64,2]{1,2,0:T(2,128)S(1)}, /*index=...) while((s32[]{:T(128)}, f32[64,2]{0,1:T(2,128)S(1)}, ...), condition=%wide.region_6.7_spmd, body=%wide.region_5.6_spmd.sunk | while | flops 49925 | bytes 466071 | solution.py:22
  274.7 0.9 fusion.74
  276.1 0.9 fusion.74
  277.4 0.9 fusion.74
  278.8 0.9 fusion.74
  280.2 0.9 fusion.74
  281.6 0.9 fusion.74
  283.0 0.9 fusion.74
  284.4 0.9 fusion.74
  285.8 0.9 fusion.74
  287.1 0.9 fusion.74
  288.5 0.9 fusion.74
  289.9 0.9 fusion.74
  291.3 0.9 fusion.74
  292.7 0.9 fusion.74
  294.1 0.9 fusion.74
  295.5 0.9 fusion.74
  298.2 0.9 fusion.74
  299.6 0.9 fusion.74
  301.0 0.9 fusion.74
  306.5 0.9 fusion.74
  307.9 0.9 fusion.74
  309.3 0.9 fusion.74
  310.7 0.9 fusion.74
  314.9 0.9 fusion.74
  316.2 0.9 fusion.74
  317.6 0.9 fusion.74
  319.0 0.9 fusion.74
  324.5 0.9 fusion.74
  325.9 0.9 fusion.74
  327.3 0.9 fusion.74
  332.9 0.9 fusion.74
  334.2 0.9 fusion.74
  335.6 0.9 fusion.74
  337.0 0.9 fusion.74
  341.2 0.9 fusion.74
  342.6 0.9 fusion.74
  343.9 0.9 fusion.74
  345.3 0.9 fusion.74
  350.9 0.9 fusion.74
  352.3 0.9 fusion.74
  353.6 0.9 fusion.74
  359.2 0.9 fusion.74
  360.6 0.9 fusion.74
  362.0 12.6 %psum.14 = f32[1,2048]{1,0:T(1,128)S(1)} all-reduce(f32[1,2048]{1,0:T(1,128)S(1)} %fusion.62), channel_id=1, replica_groups=mesh['kv'=8,'pool'=64] {'kv'}, use_global_device_ids=true, to_apply=%region_8.9 | all-reduce | flops 2048 | bytes 16384 | tf_op jit(solution)/shard_map/psum | solution.py:148
  376.2 23.6 %all_to_all.30 = bf16[1,64,32]{2,0,1:T(2,128)(2,1)S(1)} all-to-all(bf16[1,64,32]{2,0,1:T(2,128)(2,1)S(1)} %all_to_all.27), channel_id=1, replica_groups=mesh['kv'=8,'pool'=64] {'pool'}, dimensions={1} | all-to-all | bytes 8192 | tf_op jit(solution)/shard_map/all_to_all | solution.py:151
  401.1 1.3 dynamic-slice
  402.4 255.3 %all-reduce.3.cloned.1.call-done = f32[64,2048]{1,0:T(8,128)} async-done(((f32[64,2048]{1,0:T(8,128)}), f32[64,2048]{1,0:T(8,128)}) %all-reduce.3.cloned.1.call-update) | async-done | bytes 524304
  657.7 1.5 fusion.39
  659.2 80.6 %all-gather.6 = bf16[64,1,1024]{2,1,0:T(2,128)(2,1)S(1)} all-gather(bf16[1,1,1024]{2,1,0:T(2,128)(2,1)S(1)} %bitcast.153), channel_id=1, replica_groups=mesh['kv'=8,'pool'=64] {'pool'}, dimensions={0}, use_global_device_ids=true | all-gather | bytes 133120 | tf_op jit(solution)/shard_map/all_gather | solution.py:160
  739.9 23.6 %psum.15 = bf16[64,32]{0,1:T(8,128)(2,1)S(1)} all-reduce(f32[64,32]{0,1:T(8,128)S(1)} %fusion.17), channel_id=1, replica_groups=mesh['kv'=8,'pool'=64] {'kv'}, use_global_device_ids=true, to_apply=%region_11.12 | all-reduce | flops 2048 | bytes 12288 | tf_op jit(solution)/shard_map/psum | solution.py:164
  763.5 23.4 %all_to_all.31 = bf16[64,1,32]{2,1,0:T(2,128)(2,1)S(1)} all-to-all(bf16[64,1,32]{2,1,0:T(2,128)(2,1)S(1)} %copy.51), channel_id=1, replica_groups=mesh['kv'=8,'pool'=64] {'pool'}, dimensions={0} | all-to-all | bytes 8192 | tf_op jit(solution)/shard_map/all_to_all | solution.py:165
  (403 shorter events, 56.7 us)
Async XLA Ops:
  6.5 355.2 %copy-start = (bf16[256,2048]{1,0:T(8,128)(2,1)S(1)}, bf16[256,2048]{1,0:T(8,128)(2,1)}, u32[]{:S(2)}) copy-start(bf16[256,2048]{1,0:T(8,128)(2,1)} %param.18) | copy-start | bytes 3145732
  6.5 105.9 %copy-start.4 = (bf16[2048]{0:T(1024)(128)(2,1)S(1)}, bf16[2048]{0:T(1024)(128)(2,1)}, u32[]{:S(2)}) copy-start(bf16[2048]{0:T(1024)(128)(2,1)} %param.22) | copy-start | bytes 12292
  6.5 266.8 %all-gather.9.cloned.1.call-start = ((), (), s32[]{:S(2)}) async-start(), calls=%async_computation.2 | async-start | bytes 4259840 | tf_op jit(solution)/shard_map/all_gather | solution.py:16
  14.8 359.9 %copy-start.1 = (bf16[1,2048]{1,0:T(2,128)(2,1)S(1)}, bf16[1,2048]{1,0:T(2,128)(2,1)}, u32[]{:S(2)}) copy-start(bf16[1,2048]{1,0:T(2,128)(2,1)} %param.14) | copy-start | bytes 12292
  15.0 384.8 %copy-start.2 = (bf16[32,1024]{1,0:T(8,128)(2,1)S(1)}, bf16[32,1024]{1,0:T(8,128)(2,1)}, u32[]{:S(2)}) copy-start(bf16[32,1024]{1,0:T(8,128)(2,1)} %param.24) | copy-start | bytes 196612
  103.4 296.6 %copy-start.3 = (bf16[32,1024]{1,0:T(8,128)(2,1)S(1)}, bf16[32,1024]{1,0:T(8,128)(2,1)}, u32[]{:S(2)}) copy-start(bf16[32,1024]{1,0:T(8,128)(2,1)} %param.23) | copy-start | bytes 196612
  109.7 547.9 %all-reduce.3.cloned.1.call-start = ((), (), s32[]{:S(2)}) async-start(), calls=%async_computation.3 | async-start | bytes 1048576
  111.0 628.7 %copy-start.5 = (bf16[1024,32]{0,1:T(8,128)(2,1)S(1)}, bf16[1024,32]{0,1:T(8,128)(2,1)}, u32[]{:S(2)}) copy-start(bf16[1024,32]{0,1:T(8,128)(2,1)} %param.25) | copy-start | bytes 196612
Sparse Core Ops, SparseCore 0:
  109.9 140.5 all-gather.8
  401.2 256.3 all-reduce.2
where the time goes:
time: 798 us; the launch traced here: 795 us
  blocking collectives  412 us (52%)
  waiting for transfers between devices  255 us (32%)
  other arithmetic  66.5 us (8%)
  local copies, waits for them, and re-layouts  33.7 us (4%)
  between operations  15.6 us (2%)
  matrix products  8.65 us (1%)
    unnamed x3, waiting for transfers between devices  255 us
    all_gather x2, blocking collectives, combined_all(): everything = jax.tree.map(lambda part: lax.all_gather(part, axis), x)  160 us
    all_gather x1, blocking collectives, per_device(): lax.all_gather(query_rows.reshape(home_rows, query_heads * HEAD_SIZE), 'p...  88.2 us
    all_gather x1, blocking collectives, per_device(): lax.all_gather(activation, 'pool', axis=0, tiled=True)  80.6 us
    add x63, other arithmetic, combine(): early_out + late_out  55.6 us
    psum x1, blocking collectives, per_device(): mlp_out = narrow_rows(lax.psum(projected_down, 'kv'))  23.6 us
    all_to_all x1, blocking collectives, per_device(): lax.all_to_all(mlp_in, 'pool', split_axis=1, concat_axis=0, tiled=True)  23.6 us
    all_to_all x1, blocking collectives, per_device(): lax.all_to_all(mlp_out, 'pool', split_axis=0, concat_axis=1, tiled=True)  23.4 us
  transfers between devices with their start and end apart: 2, of which 1 were waited for; matrix products, arithmetic and copies ran while one was open for 1% of the time, Pallas kernels for 0%

commit v1 on v0

--- a/solution.py
+++ b/solution.py
@@ -162,7 +162,10 @@
         preferred_element_type=jnp.float32,
     )
     mlp_out = narrow_rows(lax.psum(projected_down, "kv"))
-    returned = lax.all_to_all(mlp_out, "pool", split_axis=0, concat_axis=1, tiled=True)
+    returned = jnp.concatenate(
+        lax.all_to_all(jnp.stack(jnp.split(mlp_out, lax.axis_size("pool"), axis=0)), "pool", 0, 0),
+        axis=1,
+    )
     return (residual.astype(jnp.float32) + returned.astype(jnp.float32)).astype(jnp.bfloat16)
 
 

time: 798 us -> 800 us (level)
  no operation moved by 1% of the time
where the time goes in v1:
time: 800 us; the launch traced here: 796 us
  blocking collectives  412 us (52%)
  waiting for transfers between devices  255 us (32%)
  other arithmetic  66.5 us (8%)
  local copies, waits for them, and re-layouts  35.6 us (4%)
  between operations  15.8 us (2%)
  matrix products  8.63 us (1%)
    unnamed x3, waiting for transfers between devices  255 us
    all_gather x2, blocking collectives, combined_all(): everything = jax.tree.map(lambda part: lax.all_gather(part, axis), x)  160 us
    all_gather x1, blocking collectives, per_device(): lax.all_gather(query_rows.reshape(home_rows, query_heads * HEAD_SIZE), 'p...  88.2 us
    all_gather x1, blocking collectives, per_device(): lax.all_gather(activation, 'pool', axis=0, tiled=True)  80.6 us
    add x63, other arithmetic, combine(): early_out + late_out  55.6 us
    all_to_all x1, blocking collectives, per_device(): lax.all_to_all(mlp_in, 'pool', split_axis=1, concat_axis=0, tiled=True)  23.6 us
    psum x1, blocking collectives, per_device(): mlp_out = narrow_rows(lax.psum(projected_down, 'kv'))  23.6 us
    all_to_all x1, blocking collectives, per_device(): lax.all_to_all(jnp.stack(jnp.split(mlp_out, lax.axis_size('pool'), axis=0...  23.4 us
  transfers between devices with their start and end apart: 2, of which 1 were waited for; matrix products, arithmetic and copies ran while one was open for 1% of the time, Pallas kernels for 0%

profile of v1, /device:TPU:8, one launch (start us, length us, event | category | flops | bytes accessed | tf_op | source)
XLA Modules:
  0.0 796.4 jit_solution(13739530923830120148)
XLA Ops:
  8.0 1.2 dynamic_slice.42
  10.6 1.3 multiply_reduce_fusion.1
  13.3 1.5 fusion.5
  15.0 88.2 %all-gather.3 = bf16[64,1,256]{2,1,0:T(2,128)(2,1)S(1)} all-gather(bf16[1,1,256]{2,1,0:T(2,128)(2,1)S(1)} %reshape.613), channel_id=1, replica_groups=mesh['kv'=8,'pool'=64] {'pool'}, dimensions={0}, use_global_device_ids=true | all-gather | bytes 33280 | tf_op jit(solution)/shard_map/all_gather | solution.py:85
  103.4 1.3 gather_fusion
  105.5 1.5 fusion.61
  107.5 1.3 fusion.10
  108.8 0.9 fusion.20
  109.8 1.2 convolution_bitcast_fusion.2
  111.2 1.2 fusion.4
  112.6 79.4 %all-gather.5 = f32[64,64,2]{1,2,0:T(2,128)S(1)} all-gather(f32[1,64,2]{1,2,0:T(2,128)S(1)} %convolution_bitcast_fusion), channel_id=3, replica_groups=mesh['kv'=8,'pool'=64] {'pool'}, dimensions={0}, use_global_device_ids=true | all-gather | bytes 33280 | tf_op jit(solution)/shard_map/all_gather | solution.py:16
  192.2 81.0 %all-gather.4 = f32[64,64,2]{1,2,0:T(2,128)S(1)} all-gather(f32[1,64,2]{1,2,0:T(2,128)S(1)} %bitcast.282), channel_id=2, replica_groups=mesh['kv'=8,'pool'=64] {'pool'}, dimensions={0}, use_global_device_ids=true | all-gather | bytes 33280 | tf_op jit(solution)/shard_map/all_gather | solution.py:16
  274.2 87.2 %while.19 = (s32[]{:T(128)}, f32[64,2]{0,1:T(2,128)S(1)}, f32[64,2]{0,1:T(2,128)S(1)}, f32[64,256]{1,0:T(8,128)S(1)}, f32[64,64,2]{1,2,0:T(2,128)S(1)}, /*index=...) while((s32[]{:T(128)}, f32[64,2]{0,1:T(2,128)S(1)}, ...), condition=%wide.region_6.7_spmd, body=%wide.region_5.6_spmd.sunk | while | flops 49925 | bytes 466071 | solution.py:22
  274.7 0.9 fusion.74
  276.0 0.9 fusion.74
  277.4 0.9 fusion.74
  278.8 0.9 fusion.74
  280.2 0.9 fusion.74
  281.6 0.9 fusion.74
  283.0 0.9 fusion.74
  284.4 0.9 fusion.74
  285.7 0.9 fusion.74
  287.1 0.9 fusion.74
  288.5 0.9 fusion.74
  289.9 0.9 fusion.74
  291.3 0.9 fusion.74
  292.7 0.9 fusion.74
  294.1 0.9 fusion.74
  295.4 0.9 fusion.74
  296.8 0.9 fusion.74
  298.2 0.9 fusion.74
  299.6 0.9 fusion.74
  301.0 0.9 fusion.74
  302.4 0.9 fusion.74
  303.7 0.9 fusion.74
  305.1 0.9 fusion.74
  306.5 0.9 fusion.74
  307.9 0.9 fusion.74
  309.3 0.9 fusion.74
  310.7 0.9 fusion.74
  312.1 0.9 fusion.74
  313.4 0.9 fusion.74
  314.8 0.9 fusion.74
  316.2 0.9 fusion.74
  317.6 0.9 fusion.74
  319.0 0.9 fusion.74
  320.4 0.9 fusion.74
  321.7 0.9 fusion.74
  323.1 0.9 fusion.74
  325.9 0.9 fusion.74
  334.2 0.9 fusion.74
  335.6 0.9 fusion.74
  342.5 0.9 fusion.74
  343.9 0.9 fusion.74
  352.2 0.9 fusion.74
  360.5 0.9 fusion.74
  362.0 12.6 %psum.14 = f32[1,2048]{1,0:T(1,128)S(1)} all-reduce(f32[1,2048]{1,0:T(1,128)S(1)} %fusion.62), channel_id=1, replica_groups=mesh['kv'=8,'pool'=64] {'kv'}, use_global_device_ids=true, to_apply=%region_8.9 | all-reduce | flops 2048 | bytes 16384 | tf_op jit(solution)/shard_map/psum | solution.py:148
  376.1 23.6 %all_to_all.22 = bf16[1,64,32]{2,0,1:T(2,128)(2,1)S(1)} all-to-all(bf16[1,64,32]{2,0,1:T(2,128)(2,1)S(1)} %all_to_all.19), channel_id=1, replica_groups=mesh['kv'=8,'pool'=64] {'pool'}, dimensions={1} | all-to-all | bytes 8192 | tf_op jit(solution)/shard_map/all_to_all | solution.py:151
  401.1 1.3 dynamic-slice
  402.3 255.2 %all-reduce.3.cloned.1.call-done = f32[64,2048]{1,0:T(8,128)} async-done(((f32[64,2048]{1,0:T(8,128)}), f32[64,2048]{1,0:T(8,128)}) %all-reduce.3.cloned.1.call-update) | async-done | bytes 524304
  657.6 1.5 fusion.39
  659.1 80.6 %all-gather.6 = bf16[64,1,1024]{2,1,0:T(2,128)(2,1)S(1)} all-gather(bf16[1,1,1024]{2,1,0:T(2,128)(2,1)S(1)} %bitcast.279), channel_id=1, replica_groups=mesh['kv'=8,'pool'=64] {'pool'}, dimensions={0}, use_global_device_ids=true | all-gather | bytes 133120 | tf_op jit(solution)/shard_map/all_gather | solution.py:160
  739.8 23.6 %psum.15 = bf16[64,32]{0,1:T(8,128)(2,1)S(1)} all-reduce(f32[64,32]{0,1:T(8,128)S(1)} %fusion.17), channel_id=1, replica_groups=mesh['kv'=8,'pool'=64] {'kv'}, use_global_device_ids=true, to_apply=%region_11.12 | all-reduce | flops 2048 | bytes 12288 | tf_op jit(solution)/shard_map/psum | solution.py:164
  765.4 23.4 %all_to_all.23 = bf16[64,1,32]{2,1,0:T(2,128)(2,1)S(1)} all-to-all(bf16[64,1,32]{2,1,0:T(2,128)(2,1)S(1)} %constant_dynamic-update-slice_fusion), channel_id=1, replica_groups=mesh['kv'=8,'pool'=64] {'pool'}, dimensions={0} | all-to-all | bytes 8192 | tf_op jit(solution)/shard_map/all_to_all | solution.py:166
  (470 shorter events, 58.5 us)
Async XLA Ops:
  6.5 355.2 %copy-start = (bf16[256,2048]{1,0:T(8,128)(2,1)S(1)}, bf16[256,2048]{1,0:T(8,128)(2,1)}, u32[]{:S(2)}) copy-start(bf16[256,2048]{1,0:T(8,128)(2,1)} %param.18) | copy-start | bytes 3145732
  6.5 105.9 %copy-start.4 = (bf16[2048]{0:T(1024)(128)(2,1)S(1)}, bf16[2048]{0:T(1024)(128)(2,1)}, u32[]{:S(2)}) copy-start(bf16[2048]{0:T(1024)(128)(2,1)} %param.22) | copy-start | bytes 12292
  6.5 266.8 %all-gather.9.cloned.1.call-start = ((), (), s32[]{:S(2)}) async-start(), calls=%async_computation.2 | async-start | bytes 4259840 | tf_op jit(solution)/shard_map/all_gather | solution.py:16
  14.8 359.8 %copy-start.1 = (bf16[1,2048]{1,0:T(2,128)(2,1)S(1)}, bf16[1,2048]{1,0:T(2,128)(2,1)}, u32[]{:S(2)}) copy-start(bf16[1,2048]{1,0:T(2,128)(2,1)} %param.14) | copy-start | bytes 12292
  15.0 384.8 %copy-start.2 = (bf16[32,1024]{1,0:T(8,128)(2,1)S(1)}, bf16[32,1024]{1,0:T(8,128)(2,1)}, u32[]{:S(2)}) copy-start(bf16[32,1024]{1,0:T(8,128)(2,1)} %param.24) | copy-start | bytes 196612
  103.4 296.5 %copy-start.3 = (bf16[32,1024]{1,0:T(8,128)(2,1)S(1)}, bf16[32,1024]{1,0:T(8,128)(2,1)}, u32[]{:S(2)}) copy-start(bf16[32,1024]{1,0:T(8,128)(2,1)} %param.23) | copy-start | bytes 196612
  109.7 547.8 %all-reduce.3.cloned.1.call-start = ((), (), s32[]{:S(2)}) async-start(), calls=%async_computation.3 | async-start | bytes 1048576
  111.0 628.6 %copy-start.5 = (bf16[1024,32]{0,1:T(8,128)(2,1)S(1)}, bf16[1024,32]{0,1:T(8,128)(2,1)}, u32[]{:S(2)}) copy-start(bf16[1024,32]{0,1:T(8,128)(2,1)} %param.25) | copy-start | bytes 196612
Sparse Core Ops, SparseCore 0:
  109.9 140.5 all-gather.8
  401.2 256.3 all-reduce.2
